TPU v7x, 128 devices: a whole 4x4x4 slice. The times are simulated.
128 devices in a mesh: tm: 16 (over y, x), tile: 8 (over z, core).
Axes of the slice: x: 4, y: 4, z: 4, core: 2. Of those that a mesh axis runs over, the one named last changes fastest.
Arguments:
- queries: bfloat16 [16384, 1536], P(('tm', 'tile')), may hold values from -16 to 16
- keys: bfloat16 [16384, 1536], P(('tm', 'tile')), may hold values from -16 to 16
- values: bfloat16 [16384, 1536], P(('tm', 'tile')), may hold values from -6 to 6
- grad_out: bfloat16 [16384, 1536], P(('tm', 'tile')), may hold values from -6 to 6
- span_of_group: int32 [16], replicated, may hold values from 0 to 15, each once
- noise_level: int32 [16], replicated, may hold values from 0 to 999
- next_live: int32 [128], replicated, may hold values 0 or 1
- level_bias: float32 [1000, 12], replicated, may hold values from -2 to 2
Outputs:
- attended: bfloat16 [16384, 1536], P(('tm', 'tile'))
- grad_queries: bfloat16 [16384, 1536], P(('tm', 'tile'))
- grad_keys: bfloat16 [16384, 1536], P(('tm', 'tile'))
- grad_values: bfloat16 [16384, 1536], P(('tm', 'tile'))
Inputs may be any that keep to these rules, and one draw needn't show every extreme that they name: span_of_group is a permutation of 0 to 15.
All inputs are finite; a program needn't handle non-finite values.
Results may differ from a plain program's by a relative error of at most 0.019.
Values may be sent and summed in bfloat16 or wider, within the bound.
A program may use at most 256 MiB of HBM per device.

v0:
```python
import math
import jax
import jax.numpy as jnp
from jax import lax
from jax.sharding import PartitionSpec as P


def shifted(value, axis, by):
    count = lax.axis_size(axis)
    return lax.ppermute(value, axis, [(i, (i + by) % count) for i in range(count)])


def pick_entry(table, index):
    spots = jnp.arange(table.shape[0], dtype=jnp.int32)
    return jnp.sum(jnp.where(spots == index, table, 0), axis=0)


def per_device(queries, keys, values, grad_out, span_of_group, noise_level, next_live, level_bias):
    tok_rows, model_width = queries.shape
    head_count = level_bias.shape[1]
    head_width = model_width // head_count
    inv_root = 1.0 / math.sqrt(head_width)
    groups = lax.axis_size("tm")
    tile_count = lax.axis_size("tile")
    my_group = lax.axis_index("tm")
    my_tile = lax.axis_index("tile")
    group_ids = jnp.arange(groups, dtype=jnp.int32)
    own_span = pick_entry(span_of_group, my_group)
    level_of = jnp.sum(
        jnp.where(span_of_group[:, None] == group_ids[None, :], noise_level[None, :], 0), axis=1
    )
    level_ids = jnp.arange(level_bias.shape[0], dtype=jnp.int32)
    level_table = (level_of[:, None] == level_ids[None, :]).astype(jnp.float32)
    group_bias = jnp.dot(
        level_table, level_bias, precision=lax.Precision.HIGHEST, preferred_element_type=jnp.float32
    )
    second_half = jnp.arange(2 * tok_rows, dtype=jnp.int32) >= tok_rows
    first_half = jnp.logical_not(second_half)
    live_table = next_live.reshape(groups, tile_count)
    live_here = pick_entry(next_live, my_group * tile_count + my_tile)
    attend = span_of_group <= own_span
    key_mask = attend[:, None] & (first_half[None, :] | (live_here == 1))
    near_k, near_v = shifted((keys, values), "tile", -1)
    past_k, past_v, ahead_k, ahead_v = (
        lax.all_gather(keys[None], "tm", axis=0, tiled=True),
        lax.all_gather(values[None], "tm", axis=0, tiled=True),
        lax.all_gather(near_k[None], "tm", axis=0, tiled=True),
        lax.all_gather(near_v[None], "tm", axis=0, tiled=True),
    )
    all_keys = jnp.concatenate([past_k, ahead_k], axis=1).reshape(
        groups, 2 * tok_rows, head_count, head_width
    )
    all_values = jnp.concatenate([past_v, ahead_v], axis=1).reshape(
        groups, 2 * tok_rows, head_count, head_width
    )
    query_heads = queries.reshape(tok_rows, head_count, head_width)
    grad_heads = grad_out.reshape(tok_rows, head_count, head_width)
    scores = jnp.einsum("qhe,jkhe->jhqk", query_heads, all_keys, preferred_element_type=jnp.float32)
    scores = scores * inv_root + group_bias[:, :, None, None]
    scores = jnp.where(key_mask[:, None, None, :], scores, -1e30)
    row_peak = jnp.max(scores, axis=(0, 3))
    log_total = row_peak + jnp.log(
        jnp.sum(jnp.exp(scores - row_peak[None, :, :, None]), axis=(0, 3))
    )
    weights_full = jnp.exp(scores - log_total[None, :, :, None])
    weights_low = weights_full.astype(jnp.bfloat16)
    attended = jnp.einsum(
        "jhqk,jkhe->qhe", weights_low, all_values, preferred_element_type=jnp.float32
    ).astype(jnp.bfloat16)
    row_delta = jnp.sum(grad_heads.astype(jnp.float32) * attended.astype(jnp.float32), axis=2).T
    grad_weights = jnp.einsum(
        "qhe,jkhe->jhqk", grad_heads, all_values, preferred_element_type=jnp.float32
    )
    grad_scores = (weights_full * (grad_weights - row_delta[None, :, :, None]) * inv_root).astype(
        jnp.bfloat16
    )
    grad_queries = jnp.einsum(
        "jhqk,jkhe->qhe", grad_scores, all_keys, preferred_element_type=jnp.float32
    )
    grad_queries = grad_queries.astype(jnp.bfloat16).reshape(tok_rows, model_width)
    near_q, near_g = shifted((queries, grad_out), "tile", 1)
    near_lse, near_delta = shifted((log_total, row_delta), "tile", 1)
    past_q, past_g, prev_q, prev_g = (
        lax.all_gather(queries[None], "tm", axis=0, tiled=True),
        lax.all_gather(grad_out[None], "tm", axis=0, tiled=True),
        lax.all_gather(near_q[None], "tm", axis=0, tiled=True),
        lax.all_gather(near_g[None], "tm", axis=0, tiled=True),
    )
    past_lse, past_delta, prev_lse, prev_delta = (
        lax.all_gather(log_total[None], "tm", axis=0, tiled=True),
        lax.all_gather(row_delta[None], "tm", axis=0, tiled=True),
        lax.all_gather(near_lse[None], "tm", axis=0, tiled=True),
        lax.all_gather(near_delta[None], "tm", axis=0, tiled=True),
    )
    source_q = jnp.concatenate([past_q, prev_q], axis=1).reshape(
        groups, 2 * tok_rows, head_count, head_width
    )
    source_g = jnp.concatenate([past_g, prev_g], axis=1).reshape(
        groups, 2 * tok_rows, head_count, head_width
    )
    source_lse = jnp.concatenate([past_lse, prev_lse], axis=2)
    source_delta = jnp.concatenate([past_delta, prev_delta], axis=2)
    prev_tile = (my_tile + tile_count - 1) % tile_count
    tile_ids = jnp.arange(tile_count, dtype=jnp.int32)
    prev_live = jnp.sum(jnp.where(tile_ids[None, :] == prev_tile, live_table, 0), axis=1)
    seen_by = own_span <= span_of_group
    query_mask = seen_by[:, None] & (first_half[None, :] | (prev_live[:, None] == 1))
    my_bias = jnp.sum(jnp.where(group_ids[:, None] == my_group, group_bias, 0.0), axis=0)
    key_heads = keys.reshape(tok_rows, head_count, head_width)
    value_heads = values.reshape(tok_rows, head_count, head_width)
    back_scores = jnp.einsum(
        "gqhe,khe->ghqk", source_q, key_heads, preferred_element_type=jnp.float32
    )
    back_scores = back_scores * inv_root + my_bias[None, :, None, None]
    back_full = jnp.where(
        query_mask[:, None, :, None], jnp.exp(back_scores - source_lse[:, :, :, None]), 0.0
    )
    back_low = back_full.astype(jnp.bfloat16)
    back_grad = jnp.einsum(
        "gqhe,khe->ghqk", source_g, value_heads, preferred_element_type=jnp.float32
    )
    back_ds = (back_full * (back_grad - source_delta[:, :, :, None]) * inv_root).astype(
        jnp.bfloat16
    )
    grad_keys = jnp.einsum("ghqk,gqhe->khe", back_ds, source_q, preferred_element_type=jnp.float32)
    grad_values = jnp.einsum(
        "ghqk,gqhe->khe", back_low, source_g, preferred_element_type=jnp.float32
    )
    grad_keys = grad_keys.astype(jnp.bfloat16).reshape(tok_rows, model_width)
    grad_values = grad_values.astype(jnp.bfloat16).reshape(tok_rows, model_width)
    return (attended.reshape(tok_rows, model_width), grad_queries, grad_keys, grad_values)


def solution(mesh):
    in_specs = (
        P(("tm", "tile"), None),
        P(("tm", "tile"), None),
        P(("tm", "tile"), None),
        P(("tm", "tile"), None),
        P(),
        P(),
        P(),
        P(),
    )
    out_specs = (
        P(("tm", "tile"), None),
        P(("tm", "tile"), None),
        P(("tm", "tile"), None),
        P(("tm", "tile"), None),
    )
    return jax.shard_map(
        per_device, mesh=mesh, in_specs=in_specs, out_specs=out_specs, check_vma=False
    )
```

profile of v0, /device:TPU:0, one launch (start us, length us, event | category | flops | bytes accessed | tf_op | source)
XLA Modules:
  0.0 683.0 jit_solution(12979468806883609917)
XLA Ops:
  8.0 3.6 collective-permute-start
  11.6 5.6 collective-permute-done
  17.2 0.7 copy-done.2
  18.7 3.0 collective-permute-start.1
  21.8 5.6 collective-permute-done.1
  28.8 9.1 %collective-permute-done.4 = bf16[128,1536]{1,0:T(8,128)(2,1)S(1)} collective-permute-done((bf16[128,1536]{1,0:T(8,128)(2,1)}, bf16[128,1536]{1,0:T(8,128)(2,1)S(1)}, u32[]{:S(2)}, u32[]{:S(2)}) %collective-permute-start.4) | collective-permute-done | bytes 393248 | tf_op jit(solution)/shard_map/ppermute | solution.py:10
  37.9 0.7 copy-done.3
  39.5 1.2 copy.108
  40.7 1.2 copy.103
  41.9 1.2 copy.118
  43.1 1.2 copy.113
  44.4 0.9 select_reduce_fusion.2
  46.3 1.3 fusion.55
  48.3 1.3 select_reduce_fusion.3
  49.8 1.3 broadcast_compare_fusion.1
  51.2 0.7 copy-done.4
  52.0 21.8 %all-gather.25.cloned.1.call-done = bf16[2048,1536]{1,0:T(8,128)(2,1)} async-done(((bf16[128,1536]{1,0:T(8,128)(2,1)}), bf16[2048,1536]{1,0:T(8,128)(2,1)}) %all-gather.25.cloned.1.call-update) | async-done | bytes 6291472 | tf_op jit(solution)/shard_map/all_gather | solution.py:46
  73.8 63.6 %all-gather.27.cloned.1.call-done = bf16[2048,1536]{1,0:T(8,128)(2,1)} async-done(((bf16[128,1536]{1,0:T(8,128)(2,1)}), bf16[2048,1536]{1,0:T(8,128)(2,1)}) %all-gather.27.cloned.1.call-update) | async-done | bytes 6291472 | tf_op jit(solution)/shard_map/all_gather | solution.py:48
  137.4 10.5 %pad_maximum_fusion = bf16[16,256,1536]{2,1,0:T(8,128)(2,1)} fusion(bf16[16,128,1536]{2,1,0:T(8,128)(2,1)} %bitcast.126, bf16[16,128,1536]{2,1,0:T(8,128)(2,1)} %bitcast.122), kind=kLoop, calls=%fused_computation.16 | loop fusion | flops 25165824 | bytes 25165824 | tf_op jit(solution)/shard_map/concatenate | solution.py:53
  147.9 16.7 %copy.101 = bf16[16,256,1536]{1,2,0:T(8,128)(2,1)} copy(bf16[16,256,1536]{2,1,0:T(8,128)(2,1)} %pad_maximum_fusion) | data formatting | bytes 25165824 | tf_op jit(solution)/shard_map/concatenate | solution.py:53
  164.6 35.8 %all-gather.29.cloned.1.call-done = bf16[2048,1536]{1,0:T(8,128)(2,1)} async-done(((bf16[128,1536]{1,0:T(8,128)(2,1)}), bf16[2048,1536]{1,0:T(8,128)(2,1)}) %all-gather.29.cloned.1.call-update) | async-done | bytes 6291472 | tf_op jit(solution)/shard_map/all_gather | solution.py:45
  200.4 63.5 %all-gather.31.cloned.1.call-done = bf16[2048,1536]{1,0:T(8,128)(2,1)} async-done(((bf16[128,1536]{1,0:T(8,128)(2,1)}), bf16[2048,1536]{1,0:T(8,128)(2,1)}) %all-gather.31.cloned.1.call-update) | async-done | bytes 6291472 | tf_op jit(solution)/shard_map/all_gather | solution.py:47
  263.9 10.5 %pad_maximum_fusion.1 = bf16[16,256,1536]{2,1,0:T(8,128)(2,1)} fusion(bf16[16,128,1536]{2,1,0:T(8,128)(2,1)} %bitcast.128, bf16[16,128,1536]{2,1,0:T(8,128)(2,1)} %bitcast.125), kind=kLoop, calls=%fused_computation.17 | loop fusion | flops 25165824 | bytes 25165824 | tf_op jit(solution)/shard_map/concatenate | solution.py:50
  274.3 16.7 %copy.102 = bf16[16,256,1536]{1,2,0:T(8,128)(2,1)} copy(bf16[16,256,1536]{2,1,0:T(8,128)(2,1)} %pad_maximum_fusion.1) | data formatting | bytes 25165824 | tf_op jit(solution)/shard_map/concatenate | solution.py:50
  291.1 15.8 %fusion.26 = (f32[12,128]{1,0:T(8,128)S(1)}, f32[12,16,256,128]{3,2,1,0:T(8,128)}) fusion(f32[16,12]{0,1:T(8,128)S(1)} %copy.106, pred[16,256]{1,0:T(8,128)(4,1)S(1)} %broadcast_and_fusion, bf16[128,12,128,1]{0,2,3,1:T(8,128)(2,1)S(1)} %bitcast.134, bf16[16,256,12,128]{1,3,2,0:T(8,128)(2,1)} %bitcast.118), kind=kOutput, calls=%fused_computation.36 | convolution fusion | flops 1635777024 | bytes 38152960 | tf_op jit(solution)/shard_map/qhe,jkhe->jhqk/dot_general | solution.py:58
  306.9 12.4 %exponential_reduce_fusion = f32[12,128]{1,0:T(8,128)S(1)} fusion(f32[12,128]{1,0:T(8,128)S(1)} %get-tuple-element.28, f32[16,12]{0,1:T(8,128)S(1)} %copy.106, f32[12,16,256,128]{3,2,1,0:T(8,128)} %get-tuple-element.29, pred[16,256]{1,0:T(8,128)(4,1)S(1)} %broadcast_and_fusion), kind=kLoop, calls=%fused_computation.13 | loop fusion | flops 31455744 | bytes 25182976 | tf_op jit(solution)/shard_map/reduce_sum | solution.py:63
  319.3 16.1 %multiply_reduce_fusion = (f32[128,12]{0,1:T(8,128)S(1)}, bf16[12,128,128]{2,1,0:T(8,128)(2,1)S(1)}) fusion(bf16[128,12,128]{0,2,1:T(8,128)(2,1)S(1)} %bitcast.132, bf16[16,256,12,128]{1,3,2,0:T(8,128)(2,1)} %bitcast.116, f32[12,128]{1,0:T(8,128)S(1)} %log_add_fusion, f32[16,12]{0,1:T(8,128)S(1)} %copy.106, f32[12,16,256,128]{3,2,1,0:T(8,128)} %get-tuple-element.29, ...), kind=kOutput, calls=%fused_computation.45 | convolution fusion | flops 1643051520 | bytes 38552320 | tf_op jit(solution)/shard_map/jhqk,jkhe->qhe/dot_general | solution.py:67
  335.4 1.6 collective-permute-start.5
  337.0 53.2 %all-gather.39.cloned.1.call-done = bf16[2048,1536]{1,0:T(8,128)(2,1)} async-done(((bf16[128,1536]{1,0:T(8,128)(2,1)}), bf16[2048,1536]{1,0:T(8,128)(2,1)}) %all-gather.39.cloned.1.call-update) | async-done | bytes 6291472 | tf_op jit(solution)/shard_map/all_gather | solution.py:87
  390.2 10.5 %pad_maximum_fusion.3 = bf16[16,256,1536]{2,1,0:T(8,128)(2,1)} fusion(bf16[16,128,1536]{2,1,0:T(8,128)(2,1)} %bitcast.127, bf16[16,128,1536]{2,1,0:T(8,128)(2,1)} %bitcast.123), kind=kLoop, calls=%fused_computation.19 | loop fusion | flops 25165824 | bytes 25165824 | tf_op jit(solution)/shard_map/concatenate | solution.py:98
  400.7 15.9 %copy.117 = bf16[16,256,1536]{1,2,0:T(8,128)(2,1)} copy(bf16[16,256,1536]{2,1,0:T(8,128)(2,1)} %pad_maximum_fusion.3) | data formatting | bytes 25165824 | tf_op jit(solution)/shard_map/concatenate | solution.py:98
  416.5 24.4 %all-gather.12 = f32[16,12,128]{2,1,0:T(8,128)S(1)} all-gather(f32[1,12,128]{2,1,0:T(8,128)S(1)} %bitcast.139), channel_id=8, replica_groups=mesh['tm'=16,'tile'=8] {'tm'}, dimensions={0}, use_global_device_ids=true | all-gather | bytes 104448 | tf_op jit(solution)/shard_map/all_gather | solution.py:90
  440.9 21.8 %fusion.6 = bf16[16,12,128,256]{2,3,0,1:T(8,128)(2,1)} fusion(f32[12,128]{1,0:T(8,128)S(1)} %bitcast.142, f32[12,128]{1,0:T(8,128)S(1)} %log_add_fusion, f32[16,12]{0,1:T(8,128)S(1)} %copy.106, f32[12,16,256,128]{3,2,1,0:T(8,128)} %get-tuple-element.29, pred[16,256]{1,0:T(8,128)(4,1)S(1)} %broadcast_and_fusion, bf16[128,12,128,1]{0,2,3,1:T(8,128)(2,1)S(1)} %bitcast.133, ...), kind=kOutput, calls=%fused_computation.9 | convolution fusion | flops 1660944384 | bytes 50742016 | tf_op jit(solution)/shard_map/qhe,jkhe->jhqk/dot_general | solution.py:71
  462.7 12.0 %fusion.39 = bf16[12,128,128]{2,1,0:T(8,128)(2,1)S(1)} fusion(bf16[16,256,12,128]{1,3,2,0:T(8,128)(2,1)} %bitcast.119, bf16[16,12,128,256]{2,3,0,1:T(8,128)(2,1)} %fusion.6), kind=kOutput, calls=%fused_computation.41 | convolution fusion | flops 1610809344 | bytes 25559040 | tf_op jit(solution)/shard_map/jhqk,jkhe->qhe/dot_general | solution.py:77
  474.7 42.6 %all-gather.35.cloned.1.call-done = bf16[2048,1536]{1,0:T(8,128)(2,1)} async-done(((bf16[128,1536]{1,0:T(8,128)(2,1)}), bf16[2048,1536]{1,0:T(8,128)(2,1)}) %all-gather.35.cloned.1.call-update) | async-done | bytes 6291472 | tf_op jit(solution)/shard_map/all_gather | solution.py:86
  517.3 10.4 %pad_maximum_fusion.2 = bf16[16,256,1536]{2,1,0:T(8,128)(2,1)} fusion(bf16[16,128,1536]{2,1,0:T(8,128)(2,1)} %bitcast.129, bf16[16,128,1536]{2,1,0:T(8,128)(2,1)} %bitcast.124), kind=kLoop, calls=%fused_computation.18 | loop fusion | flops 25165824 | bytes 25165824 | tf_op jit(solution)/shard_map/concatenate | solution.py:95
  527.8 13.1 %fusion.10 = f32[12,16,256,128]{3,2,1,0:T(8,128)} fusion(bf16[128,12,128,1]{0,2,3,1:T(8,128)(2,1)S(1)} %bitcast.130, bf16[16,256,12,128]{1,3,2,0:T(8,128)(2,1)} %bitcast.114), kind=kOutput, calls=%fused_computation.20 | convolution fusion | flops 1610612736 | bytes 38141952 | tf_op jit(solution)/shard_map/gqhe,khe->ghqk/dot_general | solution.py:119
  540.9 23.3 %all-gather.14 = f32[16,12,128]{2,1,0:T(8,128)S(1)} all-gather(f32[1,12,128]{2,1,0:T(8,128)S(1)} %bitcast.143), channel_id=12, replica_groups=mesh['tm'=16,'tile'=8] {'tm'}, dimensions={0}, use_global_device_ids=true | all-gather | bytes 104448 | tf_op jit(solution)/shard_map/all_gather | solution.py:91
  564.2 0.9 copy.124
  565.1 0.9 copy.125
  566.1 16.6 %copy.112 = bf16[16,256,1536]{1,2,0:T(8,128)(2,1)} copy(bf16[16,256,1536]{2,1,0:T(8,128)(2,1)} %pad_maximum_fusion.2) | data formatting | bytes 25165824 | tf_op jit(solution)/shard_map/concatenate | solution.py:95
  582.7 21.5 %all-gather.13 = f32[16,12,128]{2,1,0:T(8,128)S(1)} all-gather(f32[1,12,128]{2,1,0:T(8,128)S(1)} %bitcast.144), channel_id=9, replica_groups=mesh['tm'=16,'tile'=8] {'tm'}, dimensions={0}, use_global_device_ids=true | all-gather | bytes 104448 | tf_op jit(solution)/shard_map/all_gather | solution.py:92
  604.4 23.3 %all-gather.15 = f32[16,12,128]{2,1,0:T(8,128)S(1)} all-gather(f32[1,12,128]{2,1,0:T(8,128)S(1)} %bitcast.140), channel_id=13, replica_groups=mesh['tm'=16,'tile'=8] {'tm'}, dimensions={0}, use_global_device_ids=true | all-gather | bytes 104448 | tf_op jit(solution)/shard_map/all_gather | solution.py:93
  627.8 23.3 %fusion.9 = (bf16[16,12,256,128]{3,2,0,1:T(8,128)(2,1)}, bf16[16,12,256,128]{3,2,0,1:T(8,128)(2,1)}) fusion(f32[16,12,256]{2,0,1:T(8,128)S(1)} %copy.116, f32[12]{0:T(128)S(1)} %get-tuple-element.32, pred[16,256]{1,0:T(8,128)(4,1)S(1)} %or_and_fusion, f32[16,12,256]{2,0,1:T(8,128)S(1)} %copy.121, f32[12,16,256,128]{3,2,1,0:T(8,128)} %fusion.10, ...), kind=kOutput, calls=%fused_computation.15 | convolution fusion | flops 1667235840 | bytes 63705136 | tf_op jit(solution)/shard_map/gqhe,khe->ghqk/dot_general | solution.py:111
  651.1 11.6 %fusion.48 = bf16[12,128,128]{2,1,0:T(8,128)(2,1)S(1)} fusion(bf16[16,256,12,128]{1,3,2,0:T(8,128)(2,1)} %bitcast.121, bf16[16,12,256,128]{3,2,0,1:T(8,128)(2,1)} %get-tuple-element.25), kind=kOutput, calls=%fused_computation.44 | convolution fusion | flops 1610809344 | bytes 25559040 | tf_op jit(solution)/shard_map/ghqk,gqhe->khe/dot_general | solution.py:125
  662.7 0.9 copy.126
  663.6 11.6 %fusion.45 = bf16[12,128,128]{2,1,0:T(8,128)(2,1)S(1)} fusion(bf16[16,256,12,128]{1,3,2,0:T(8,128)(2,1)} %bitcast.115, bf16[16,12,256,128]{3,2,0,1:T(8,128)(2,1)} %get-tuple-element.24), kind=kOutput, calls=%fused_computation.43 | convolution fusion | flops 1610809344 | bytes 25559040 | tf_op jit(solution)/shard_map/ghqk,gqhe->khe/dot_general | solution.py:126
  675.2 0.9 copy.127
  (49 shorter events, 5.5 us)
Async XLA Ops:
  7.2 38.1 %copy-start = (f32[1000,12]{0,1:T(8,128)S(1)}, f32[1000,12]{0,1:T(8,128)}, u32[]{:S(2)}) copy-start(f32[1000,12]{0,1:T(8,128)} %param.15) | copy-start | bytes 144004
  7.2 66.6 %all-gather.25.cloned.1.call-start = ((), (), s32[]{:S(2)}) async-start(), calls=%async_computation | async-start | bytes 6684672 | tf_op jit(solution)/shard_map/all_gather | solution.py:46
  7.9 129.5 %all-gather.27.cloned.1.call-start = ((), (), s32[]{:S(2)}) async-start(), calls=%async_computation.1 | async-start | bytes 6684672 | tf_op jit(solution)/shard_map/all_gather | solution.py:48
  8.0 9.2 %collective-permute-start = (bf16[128,1536]{1,0:T(8,128)(2,1)}, bf16[128,1536]{1,0:T(8,128)(2,1)S(1)}, u32[]{:S(2)}, u32[]{:S(2)}) collective-permute-start(bf16[128,1536]{1,0:T(8,128)(2,1)} %param.10), channel_id=1, source_target_pairs={{0,7},{1,0},{2,1},{3,2},{4,3},{5,4},{6,5},{7,6},{8,15},{9,8},{10,9... | collective-permute-start | bytes 1179656 | tf_op jit(solution)/shard_map/ppermute | solution.py:10
  17.2 0.7 copy-start.2
  17.9 182.5 %all-gather.29.cloned.1.call-start = ((), (), s32[]{:S(2)}) async-start(), calls=%async_computation.2 | async-start | bytes 6684672 | tf_op jit(solution)/shard_map/all_gather | solution.py:45
  18.7 245.2 %all-gather.31.cloned.1.call-start = ((), (), s32[]{:S(2)}) async-start(), calls=%async_computation.3 | async-start | bytes 6684672 | tf_op jit(solution)/shard_map/all_gather | solution.py:47
  18.7 8.6 %collective-permute-start.1 = (bf16[128,1536]{1,0:T(8,128)(2,1)}, bf16[128,1536]{1,0:T(8,128)(2,1)S(1)}, u32[]{:S(2)}, u32[]{:S(2)}) collective-permute-start(bf16[128,1536]{1,0:T(8,128)(2,1)} %param.9), channel_id=1, source_target_pairs={{0,7},{1,0},{2,1},{3,2},{4,3},{5,4},{6,5},{7,6},{8,15},{9,8},{10,9... | collective-permute-start | bytes 1179656 | tf_op jit(solution)/shard_map/ppermute | solution.py:10
  27.4 0.7 copy-start.5
  28.1 308.9 %all-gather.37.cloned.1.call-start = ((), (), s32[]{:S(2)}) async-start(), calls=%async_computation.6 | async-start | bytes 6684672 | tf_op jit(solution)/shard_map/all_gather | solution.py:85
  28.7 361.5 %all-gather.39.cloned.1.call-start = ((), (), s32[]{:S(2)}) async-start(), calls=%async_computation.7 | async-start | bytes 6684672 | tf_op jit(solution)/shard_map/all_gather | solution.py:87
  28.8 9.1 %collective-permute-start.4 = (bf16[128,1536]{1,0:T(8,128)(2,1)}, bf16[128,1536]{1,0:T(8,128)(2,1)S(1)}, u32[]{:S(2)}, u32[]{:S(2)}) collective-permute-start(bf16[128,1536]{1,0:T(8,128)(2,1)} %param.11), channel_id=1, source_target_pairs={{0,1},{1,2},{2,3},{3,4},{4,5},{5,6},{6,7},{7,0},{8,9},{9,10},{10,1... | collective-permute-start | bytes 1179656 | tf_op jit(solution)/shard_map/ppermute | solution.py:10
  37.9 0.7 copy-start.3
  38.6 436.1 %all-gather.33.cloned.1.call-start = ((), (), s32[]{:S(2)}) async-start(), calls=%async_computation.4 | async-start | bytes 6684672 | tf_op jit(solution)/shard_map/all_gather | solution.py:84
  39.4 478.0 %all-gather.35.cloned.1.call-start = ((), (), s32[]{:S(2)}) async-start(), calls=%async_computation.5 | async-start | bytes 6684672 | tf_op jit(solution)/shard_map/all_gather | solution.py:86
  39.4 11.8 %collective-permute-start.2 = (bf16[128,1536]{1,0:T(8,128)(2,1)}, bf16[128,1536]{1,0:T(8,128)(2,1)S(1)}, u32[]{:S(2)}, u32[]{:S(2)}) collective-permute-start(bf16[128,1536]{1,0:T(8,128)(2,1)} %param.8), channel_id=1, source_target_pairs={{0,1},{1,2},{2,3},{3,4},{4,5},{5,6},{6,7},{7,0},{8,9},{9,10},{10,1... | collective-permute-start | bytes 1179656 | tf_op jit(solution)/shard_map/ppermute | solution.py:10
  51.2 0.7 copy-start.4
  319.3 263.5 %collective-permute-start.3 = (f32[12,128]{1,0:T(8,128)S(1)}, f32[12,128]{1,0:T(8,128)S(1)}, u32[]{:S(2)}, u32[]{:S(2)}) collective-permute-start(f32[12,128]{1,0:T(8,128)S(1)} %log_add_fusion), channel_id=1, source_target_pairs={{0,1},{1,2},{2,3},{3,4},{4,5},{5,6},{6,7},{7,0},{8,9},{9,10},{10,1... | collective-permute-start | bytes 18440 | tf_op jit(solution)/shard_map/ppermute | solution.py:10
  335.4 269.0 %collective-permute-start.5 = (f32[12,128]{1,0:T(8,128)S(1)}, f32[12,128]{1,0:T(8,128)S(1)}, u32[]{:S(2)}, u32[]{:S(2)}) collective-permute-start(f32[12,128]{1,0:T(8,128)S(1)} %bitcast.141), channel_id=1, source_target_pairs={{0,1},{1,2},{2,3},{3,4},{4,5},{5,6},{6,7},{7,0},{8,9},{9,10},{10,1... | collective-permute-start | bytes 18440 | tf_op jit(solution)/shard_map/ppermute | solution.py:10
  663.6 12.6 %copy-start.1 = (f32[1000,12]{0,1:T(8,128)S(1)}, f32[1000,12]{0,1:T(8,128)}, u32[]{:S(2)}) copy-start(f32[1000,12]{0,1:T(8,128)} %param.15) | copy-start | bytes 144004
Sparse Core Ops, SparseCore 0:
  10.1 63.6 all-gather.24
  76.5 60.8 all-gather.26
  139.5 60.8 all-gather.28
  203.0 60.8 all-gather.30
  265.8 60.8 all-gather.36
  329.3 60.8 all-gather.38
  392.3 61.3 all-gather.32
  456.5 60.8 all-gather.34
where the time goes:
time: 685 us; the launch traced here: 683 us
  waiting for transfers between devices  303 us (44%)
  matrix products  125 us (18%)
  blocking collectives  92.5 us (14%)
  local copies, waits for them, and re-layouts  78.6 us (11%)
  other arithmetic  59.4 us (9%)
  between operations  15 us (2%)
  starting transfers between devices  8.61 us (1%)
    all_gather x1, waiting for transfers between devices, per_device(): lax.all_gather(near_v[None], 'tm', axis=0, tiled=True)  63.6 us
    all_gather x1, waiting for transfers between devices, per_device(): lax.all_gather(near_k[None], 'tm', axis=0, tiled=True)  63.5 us
    all_gather x1, waiting for transfers between devices, per_device(): lax.all_gather(near_g[None], 'tm', axis=0, tiled=True)  53.2 us
    all_gather x1, waiting for transfers between devices, per_device(): lax.all_gather(near_q[None], 'tm', axis=0, tiled=True)  42.6 us
    all_gather x1, waiting for transfers between devices, per_device(): lax.all_gather(keys[None], 'tm', axis=0, tiled=True)  35.8 us
    all_gather x1, blocking collectives, per_device(): lax.all_gather(log_total[None], 'tm', axis=0, tiled=True)  24.4 us
    all_gather x1, blocking collectives, per_device(): lax.all_gather(row_delta[None], 'tm', axis=0, tiled=True)  23.3 us
    all_gather x1, blocking collectives, per_device(): lax.all_gather(near_delta[None], 'tm', axis=0, tiled=True)  23.3 us
  transfers between devices with their start and end apart: 14, of which 9 were waited for; matrix products, arithmetic and copies ran while one was open for 31% of the time, Pallas kernels for 0%

commit v1 on v0

--- a/solution.py
+++ b/solution.py
@@ -1,8 +1,21 @@
+import functools
 import math
 import jax
 import jax.numpy as jnp
 from jax import lax
 from jax.sharding import PartitionSpec as P
+
+
+def handle_yards(vals, axis_no):
+    views = []
+    for _ in range(lax.axis_size("tm")):
+        views.append(vals)
+    outcome_arr = jnp.concatenate(views, axis_no)
+    aux = lax.all_to_all(outcome_arr, "tm", split_axis=axis_no, concat_axis=axis_no, tiled=True)
+    return aux
+
+
+panels_close = functools.partial(handle_yards, axis_no=0)
 
 
 def shifted(value, axis, by):
@@ -43,7 +56,7 @@
     near_k, near_v = shifted((keys, values), "tile", -1)
     past_k, past_v, ahead_k, ahead_v = (
         lax.all_gather(keys[None], "tm", axis=0, tiled=True),
-        lax.all_gather(values[None], "tm", axis=0, tiled=True),
+        panels_close(values[None]),
         lax.all_gather(near_k[None], "tm", axis=0, tiled=True),
         lax.all_gather(near_v[None], "tm", axis=0, tiled=True),
     )

time: 685 us -> 696 us (1.016)
  waiting for transfers between devices: 303 us -> 310 us
  starting transfers between devices: 8.61 us -> 15.6 us
    all_to_all x0 -> x1, waiting for transfers between devices: none -> 88.4 us  [handle_yards(): lax.all_to_all(outcome_arr, 'tm', split_axis=axis_no, concat_axis=axis_no...]
    all_gather x1, waiting for transfers between devices: 63.6 us -> 0.01 us  [per_device(): lax.all_gather(near_v[None], 'tm', axis=0, tiled=True)]
    all_gather x1 -> x0, waiting for transfers between devices: 21.8 us -> none  [per_device(): lax.all_gather(values[None], 'tm', axis=0, tiled=True)]
    all_to_all x0 -> x1, starting transfers between devices: none -> 7.08 us  [handle_yards(): lax.all_to_all(outcome_arr, 'tm', split_axis=axis_no, concat_axis=axis_no...]
  transfers between devices with their start and end apart: 14 -> 14, of which waited for: 9 -> 9; matrix products, arithmetic and copies ran while one was open for 31% -> 30% of each run, Pallas kernels for 0% -> 0%
where the time goes in v1:
time: 696 us; the launch traced here: 694 us
  waiting for transfers between devices  310 us (45%)
  matrix products  125 us (18%)
  blocking collectives  93 us (13%)
  local copies, waits for them, and re-layouts  78.1 us (11%)
  other arithmetic  56.6 us (8%)
  starting transfers between devices  15.6 us (2%)
  between operations  15.1 us (2%)
    all_to_all x1, waiting for transfers between devices, handle_yards(): lax.all_to_all(outcome_arr, 'tm', split_axis=axis_no, concat_axis=axis_no...  88.4 us
    all_gather x1, waiting for transfers between devices, per_device(): lax.all_gather(near_k[None], 'tm', axis=0, tiled=True)  63.6 us
    all_gather x1, waiting for transfers between devices, per_device(): lax.all_gather(near_g[None], 'tm', axis=0, tiled=True)  53.3 us
    all_gather x1, waiting for transfers between devices, per_device(): lax.all_gather(near_q[None], 'tm', axis=0, tiled=True)  42 us
    all_gather x1, waiting for transfers between devices, per_device(): lax.all_gather(keys[None], 'tm', axis=0, tiled=True)  37.2 us
    all_gather x1, blocking collectives, per_device(): lax.all_gather(log_total[None], 'tm', axis=0, tiled=True)  24.9 us
    ppermute x6, waiting for transfers between devices, shifted(): lax.ppermute(value, axis, [(i, (i + by) % count) for i in range(count)])  23.8 us
    all_gather x1, blocking collectives, per_device(): lax.all_gather(row_delta[None], 'tm', axis=0, tiled=True)  23.3 us
  transfers between devices with their start and end apart: 14, of which 9 were waited for; matrix products, arithmetic and copies ran while one was open for 30% of the time, Pallas kernels for 0%

profile of v1, /device:TPU:0, one launch (start us, length us, event | category | flops | bytes accessed | tf_op | source)
XLA Modules:
  0.0 694.1 jit_solution(11319764645234005324)
XLA Ops:
  7.3 3.6 collective-permute-start
  10.9 5.6 collective-permute-done
  16.5 0.7 copy-done.6
  17.3 0.7 all-gather.25.cloned.1.call-update
  18.1 3.0 collective-permute-start.1
  21.1 5.6 collective-permute-done.1
  26.7 0.7 copy-done.8
  27.5 0.5 all-gather.33.cloned.1.call-update
  28.1 8.7 %collective-permute-done.4 = bf16[128,1536]{1,0:T(8,128)(2,1)S(1)} collective-permute-done((bf16[128,1536]{1,0:T(8,128)(2,1)}, bf16[128,1536]{1,0:T(8,128)(2,1)S(1)}, u32[]{:S(2)}, u32[]{:S(2)}) %collective-permute-start.4) | collective-permute-done | bytes 393248 | tf_op jit(solution)/shard_map/ppermute | solution.py:23
  36.8 0.7 copy-done.7
  38.2 4.3 concatenate.21
  42.4 7.1 %all-to-all-start = ((bf16[16,128,1536]{2,1,0:T(8,128)(2,1)}), bf16[16,128,1536]{2,1,0:T(8,128)(2,1)}, u32[]{:S(2)}, u32[]{:S(2)}) async-start(bf16[16,128,1536]{2,1,0:T(8,128)(2,1)} %concatenate.21), calls=%async_computation | async-start | bytes 12582912 | tf_op jit(solution)/shard_map/all_to_all | solution.py:14
  51.2 0.7 fusion.55
  52.5 0.6 select_reduce_fusion.3
  53.3 0.7 broadcast_compare_fusion.1
  54.1 3.9 collective-permute-done.2
  58.0 0.7 copy-done.9
  58.8 88.4 %all-to-all-done = bf16[16,128,1536]{2,1,0:T(8,128)(2,1)} async-done(((bf16[16,128,1536]{2,1,0:T(8,128)(2,1)}), bf16[16,128,1536]{2,1,0:T(8,128)(2,1)}, u32[]{:S(2)}, u32[]{:S(2)}) %all-to-all-start) | async-done | bytes 6291488 | tf_op jit(solution)/shard_map/all_to_all | solution.py:14
  147.2 10.4 %pad_maximum_fusion = bf16[16,256,1536]{2,1,0:T(8,128)(2,1)} fusion(bf16[16,128,1536]{2,1,0:T(8,128)(2,1)} %bitcast.124, bf16[16,128,1536]{2,1,0:T(8,128)(2,1)} %all-to-all-done), kind=kLoop, calls=%fused_computation.16 | loop fusion | flops 25165824 | bytes 25165824 | tf_op jit(solution)/shard_map/concatenate | solution.py:66
  157.6 16.7 %copy.102 = bf16[16,256,1536]{1,2,0:T(8,128)(2,1)} copy(bf16[16,256,1536]{2,1,0:T(8,128)(2,1)} %pad_maximum_fusion) | data formatting | bytes 25165824 | tf_op jit(solution)/shard_map/concatenate | solution.py:66
  174.3 37.2 %all-gather.25.cloned.1.call-done = bf16[2048,1536]{1,0:T(8,128)(2,1)} async-done(((bf16[128,1536]{1,0:T(8,128)(2,1)}), bf16[2048,1536]{1,0:T(8,128)(2,1)}) %all-gather.25.cloned.1.call-update) | async-done | bytes 6291472 | tf_op jit(solution)/shard_map/all_gather | solution.py:58
  211.5 63.6 %all-gather.27.cloned.1.call-done = bf16[2048,1536]{1,0:T(8,128)(2,1)} async-done(((bf16[128,1536]{1,0:T(8,128)(2,1)}), bf16[2048,1536]{1,0:T(8,128)(2,1)}) %all-gather.27.cloned.1.call-update) | async-done | bytes 6291472 | tf_op jit(solution)/shard_map/all_gather | solution.py:60
  275.1 10.4 %pad_maximum_fusion.1 = bf16[16,256,1536]{2,1,0:T(8,128)(2,1)} fusion(bf16[16,128,1536]{2,1,0:T(8,128)(2,1)} %bitcast.126, bf16[16,128,1536]{2,1,0:T(8,128)(2,1)} %bitcast.123), kind=kLoop, calls=%fused_computation.17 | loop fusion | flops 25165824 | bytes 25165824 | tf_op jit(solution)/shard_map/concatenate | solution.py:63
  285.6 16.7 %copy.103 = bf16[16,256,1536]{1,2,0:T(8,128)(2,1)} copy(bf16[16,256,1536]{2,1,0:T(8,128)(2,1)} %pad_maximum_fusion.1) | data formatting | bytes 25165824 | tf_op jit(solution)/shard_map/concatenate | solution.py:63
  302.3 15.8 %fusion.26 = (f32[12,128]{1,0:T(8,128)S(1)}, f32[12,16,256,128]{3,2,1,0:T(8,128)}) fusion(f32[16,12]{0,1:T(8,128)S(1)} %copy.107, pred[16,256]{1,0:T(8,128)(4,1)S(1)} %broadcast_and_fusion, bf16[128,12,128,1]{0,2,3,1:T(8,128)(2,1)S(1)} %bitcast.132, bf16[16,256,12,128]{1,3,2,0:T(8,128)(2,1)} %bitcast.117), kind=kOutput, calls=%fused_computation.36 | convolution fusion | flops 1635777024 | bytes 38152960 | tf_op jit(solution)/shard_map/qhe,jkhe->jhqk/dot_general | solution.py:71
  318.0 12.4 %exponential_reduce_fusion = f32[12,128]{1,0:T(8,128)S(1)} fusion(f32[12,128]{1,0:T(8,128)S(1)} %get-tuple-element.28, f32[16,12]{0,1:T(8,128)S(1)} %copy.107, f32[12,16,256,128]{3,2,1,0:T(8,128)} %get-tuple-element.29, pred[16,256]{1,0:T(8,128)(4,1)S(1)} %broadcast_and_fusion), kind=kLoop, calls=%fused_computation.13 | loop fusion | flops 31455744 | bytes 25182976 | tf_op jit(solution)/shard_map/reduce_sum | solution.py:76
  330.4 16.1 %multiply_reduce_fusion = (f32[128,12]{0,1:T(8,128)S(1)}, bf16[12,128,128]{2,1,0:T(8,128)(2,1)S(1)}) fusion(bf16[128,12,128]{0,2,1:T(8,128)(2,1)S(1)} %bitcast.130, bf16[16,256,12,128]{1,3,2,0:T(8,128)(2,1)} %bitcast.115, f32[12,128]{1,0:T(8,128)S(1)} %log_add_fusion, f32[16,12]{0,1:T(8,128)S(1)} %copy.107, f32[12,16,256,128]{3,2,1,0:T(8,128)} %get-tuple-element.29, ...), kind=kOutput, calls=%fused_computation.45 | convolution fusion | flops 1643051520 | bytes 38552320 | tf_op jit(solution)/shard_map/jhqk,jkhe->qhe/dot_general | solution.py:80
  346.5 1.6 collective-permute-start.5
  348.2 53.3 %all-gather.35.cloned.1.call-done = bf16[2048,1536]{1,0:T(8,128)(2,1)} async-done(((bf16[128,1536]{1,0:T(8,128)(2,1)}), bf16[2048,1536]{1,0:T(8,128)(2,1)}) %all-gather.35.cloned.1.call-update) | async-done | bytes 6291472 | tf_op jit(solution)/shard_map/all_gather | solution.py:100
  401.5 10.5 %pad_maximum_fusion.3 = bf16[16,256,1536]{2,1,0:T(8,128)(2,1)} fusion(bf16[16,128,1536]{2,1,0:T(8,128)(2,1)} %bitcast.125, bf16[16,128,1536]{2,1,0:T(8,128)(2,1)} %bitcast.121), kind=kLoop, calls=%fused_computation.19 | loop fusion | flops 25165824 | bytes 25165824 | tf_op jit(solution)/shard_map/concatenate | solution.py:111
  411.9 15.8 %copy.118 = bf16[16,256,1536]{1,2,0:T(8,128)(2,1)} copy(bf16[16,256,1536]{2,1,0:T(8,128)(2,1)} %pad_maximum_fusion.3) | data formatting | bytes 25165824 | tf_op jit(solution)/shard_map/concatenate | solution.py:111
  427.8 24.9 %all-gather.11 = f32[16,12,128]{2,1,0:T(8,128)S(1)} all-gather(f32[1,12,128]{2,1,0:T(8,128)S(1)} %bitcast.137), channel_id=7, replica_groups=mesh['tm'=16,'tile'=8] {'tm'}, dimensions={0}, use_global_device_ids=true | all-gather | bytes 104448 | tf_op jit(solution)/shard_map/all_gather | solution.py:103
  452.7 21.8 %fusion.6 = bf16[16,12,128,256]{2,3,0,1:T(8,128)(2,1)} fusion(f32[12,128]{1,0:T(8,128)S(1)} %bitcast.140, f32[12,128]{1,0:T(8,128)S(1)} %log_add_fusion, f32[16,12]{0,1:T(8,128)S(1)} %copy.107, f32[12,16,256,128]{3,2,1,0:T(8,128)} %get-tuple-element.29, pred[16,256]{1,0:T(8,128)(4,1)S(1)} %broadcast_and_fusion, bf16[128,12,128,1]{0,2,3,1:T(8,128)(2,1)S(1)} %bitcast.131, ...), kind=kOutput, calls=%fused_computation.9 | convolution fusion | flops 1660944384 | bytes 50742016 | tf_op jit(solution)/shard_map/qhe,jkhe->jhqk/dot_general | solution.py:84
  474.5 12.0 %fusion.39 = bf16[12,128,128]{2,1,0:T(8,128)(2,1)S(1)} fusion(bf16[16,256,12,128]{1,3,2,0:T(8,128)(2,1)} %bitcast.118, bf16[16,12,128,256]{2,3,0,1:T(8,128)(2,1)} %fusion.6), kind=kOutput, calls=%fused_computation.41 | convolution fusion | flops 1610809344 | bytes 25559040 | tf_op jit(solution)/shard_map/jhqk,jkhe->qhe/dot_general | solution.py:90
  486.5 42.0 %all-gather.31.cloned.1.call-done = bf16[2048,1536]{1,0:T(8,128)(2,1)} async-done(((bf16[128,1536]{1,0:T(8,128)(2,1)}), bf16[2048,1536]{1,0:T(8,128)(2,1)}) %all-gather.31.cloned.1.call-update) | async-done | bytes 6291472 | tf_op jit(solution)/shard_map/all_gather | solution.py:99
  528.5 10.4 %pad_maximum_fusion.2 = bf16[16,256,1536]{2,1,0:T(8,128)(2,1)} fusion(bf16[16,128,1536]{2,1,0:T(8,128)(2,1)} %bitcast.127, bf16[16,128,1536]{2,1,0:T(8,128)(2,1)} %bitcast.122), kind=kLoop, calls=%fused_computation.18 | loop fusion | flops 25165824 | bytes 25165824 | tf_op jit(solution)/shard_map/concatenate | solution.py:108
  538.9 13.1 %fusion.10 = f32[12,16,256,128]{3,2,1,0:T(8,128)} fusion(bf16[128,12,128,1]{0,2,3,1:T(8,128)(2,1)S(1)} %bitcast.128, bf16[16,256,12,128]{1,3,2,0:T(8,128)(2,1)} %bitcast.113), kind=kOutput, calls=%fused_computation.20 | convolution fusion | flops 1610612736 | bytes 38141952 | tf_op jit(solution)/shard_map/gqhe,khe->ghqk/dot_general | solution.py:132
  552.0 23.3 %all-gather.13 = f32[16,12,128]{2,1,0:T(8,128)S(1)} all-gather(f32[1,12,128]{2,1,0:T(8,128)S(1)} %bitcast.141), channel_id=11, replica_groups=mesh['tm'=16,'tile'=8] {'tm'}, dimensions={0}, use_global_device_ids=true | all-gather | bytes 104448 | tf_op jit(solution)/shard_map/all_gather | solution.py:104
  575.4 0.9 copy.125
  576.3 0.9 copy.126
  577.2 16.6 %copy.113 = bf16[16,256,1536]{1,2,0:T(8,128)(2,1)} copy(bf16[16,256,1536]{2,1,0:T(8,128)(2,1)} %pad_maximum_fusion.2) | data formatting | bytes 25165824 | tf_op jit(solution)/shard_map/concatenate | solution.py:108
  593.9 21.5 %all-gather.12 = f32[16,12,128]{2,1,0:T(8,128)S(1)} all-gather(f32[1,12,128]{2,1,0:T(8,128)S(1)} %bitcast.142), channel_id=8, replica_groups=mesh['tm'=16,'tile'=8] {'tm'}, dimensions={0}, use_global_device_ids=true | all-gather | bytes 104448 | tf_op jit(solution)/shard_map/all_gather | solution.py:105
  615.5 23.3 %all-gather.14 = f32[16,12,128]{2,1,0:T(8,128)S(1)} all-gather(f32[1,12,128]{2,1,0:T(8,128)S(1)} %bitcast.138), channel_id=12, replica_groups=mesh['tm'=16,'tile'=8] {'tm'}, dimensions={0}, use_global_device_ids=true | all-gather | bytes 104448 | tf_op jit(solution)/shard_map/all_gather | solution.py:106
  639.0 23.2 %fusion.9 = (bf16[16,12,256,128]{3,2,0,1:T(8,128)(2,1)}, bf16[16,12,256,128]{3,2,0,1:T(8,128)(2,1)}) fusion(f32[16,12,256]{2,0,1:T(8,128)S(1)} %copy.117, f32[12]{0:T(128)S(1)} %get-tuple-element.32, pred[16,256]{1,0:T(8,128)(4,1)S(1)} %or_and_fusion, f32[16,12,256]{2,0,1:T(8,128)S(1)} %copy.122, f32[12,16,256,128]{3,2,1,0:T(8,128)} %fusion.10, ...), kind=kOutput, calls=%fused_computation.15 | convolution fusion | flops 1667235840 | bytes 63705136 | tf_op jit(solution)/shard_map/gqhe,khe->ghqk/dot_general | solution.py:124
  662.2 11.6 %fusion.48 = bf16[12,128,128]{2,1,0:T(8,128)(2,1)S(1)} fusion(bf16[16,256,12,128]{1,3,2,0:T(8,128)(2,1)} %bitcast.120, bf16[16,12,256,128]{3,2,0,1:T(8,128)(2,1)} %get-tuple-element.25), kind=kOutput, calls=%fused_computation.44 | convolution fusion | flops 1610809344 | bytes 25559040 | tf_op jit(solution)/shard_map/ghqk,gqhe->khe/dot_general | solution.py:138
  673.7 0.9 copy.127
  674.7 11.6 %fusion.45 = bf16[12,128,128]{2,1,0:T(8,128)(2,1)S(1)} fusion(bf16[16,256,12,128]{1,3,2,0:T(8,128)(2,1)} %bitcast.114, bf16[16,12,256,128]{3,2,0,1:T(8,128)(2,1)} %get-tuple-element.24), kind=kOutput, calls=%fused_computation.43 | convolution fusion | flops 1610809344 | bytes 25559040 | tf_op jit(solution)/shard_map/ghqk,gqhe->khe/dot_general | solution.py:139
  686.3 0.9 copy.128
  (63 shorter events, 3.0 us)
Async XLA Ops:
  7.2 43.6 %copy-start = (f32[1000,12]{0,1:T(8,128)S(1)}, f32[1000,12]{0,1:T(8,128)}, u32[]{:S(2)}) copy-start(f32[1000,12]{0,1:T(8,128)} %param.15) | copy-start | bytes 144004
  7.2 42.9 %copy-start.2 = (bf16[128,1536]{1,0:T(8,128)(2,1)S(1)}, bf16[128,1536]{1,0:T(8,128)(2,1)}, u32[]{:S(2)}) copy-start(bf16[128,1536]{1,0:T(8,128)(2,1)} %param.10) | copy-start | bytes 1179652
  7.2 43.1 %copy-start.3 = (bf16[128,1536]{1,0:T(8,128)(2,1)S(1)}, bf16[128,1536]{1,0:T(8,128)(2,1)}, u32[]{:S(2)}) copy-start(bf16[128,1536]{1,0:T(8,128)(2,1)} %param.9) | copy-start | bytes 1179652
  7.2 42.4 %copy-start.4 = (bf16[128,1536]{1,0:T(8,128)(2,1)S(1)}, bf16[128,1536]{1,0:T(8,128)(2,1)}, u32[]{:S(2)}) copy-start(bf16[128,1536]{1,0:T(8,128)(2,1)} %param.11) | copy-start | bytes 1179652
  7.2 42.3 %copy-start.5 = (bf16[128,1536]{1,0:T(8,128)(2,1)S(1)}, bf16[128,1536]{1,0:T(8,128)(2,1)}, u32[]{:S(2)}) copy-start(bf16[128,1536]{1,0:T(8,128)(2,1)} %param.8) | copy-start | bytes 1179652
  7.2 43.3 %copy-start.12 = (s32[16]{0:T(128)S(1)}, s32[16]{0:T(128)}, u32[]{:S(2)}) copy-start(s32[16]{0:T(128)} %param.13) | copy-start | bytes 196
  7.2 43.3 %copy-start.11 = (s32[16]{0:T(128)S(1)}, s32[16]{0:T(128)}, u32[]{:S(2)}) copy-start(s32[16]{0:T(128)} %param.12) | copy-start | bytes 196
  7.2 43.8 %copy-start.10 = (s32[128]{0:T(128)S(1)}, s32[128]{0:T(128)}, u32[]{:S(2)}) copy-start(s32[128]{0:T(128)} %param.14) | copy-start | bytes 1540
  7.3 139.9 %all-gather.23.cloned.1.call-start = ((), (), s32[]{:S(2)}) async-start(), calls=%async_computation.1 | async-start | bytes 6684672 | tf_op jit(solution)/shard_map/all_gather | solution.py:61
  7.3 9.2 %collective-permute-start = (bf16[128,1536]{1,0:T(8,128)(2,1)}, bf16[128,1536]{1,0:T(8,128)(2,1)S(1)}, u32[]{:S(2)}, u32[]{:S(2)}) collective-permute-start(bf16[128,1536]{1,0:T(8,128)(2,1)} %param.10), channel_id=1, source_target_pairs={{0,7},{1,0},{2,1},{3,2},{4,3},{5,4},{6,5},{7,6},{8,15},{9,8},{10,9... | collective-permute-start | bytes 1179656 | tf_op jit(solution)/shard_map/ppermute | solution.py:23
  16.5 0.7 copy-start.6
  17.3 194.3 %all-gather.25.cloned.1.call-start = ((), (), s32[]{:S(2)}) async-start(), calls=%async_computation.2 | async-start | bytes 6684672 | tf_op jit(solution)/shard_map/all_gather | solution.py:58
  18.0 257.1 %all-gather.27.cloned.1.call-start = ((), (), s32[]{:S(2)}) async-start(), calls=%async_computation.3 | async-start | bytes 6684672 | tf_op jit(solution)/shard_map/all_gather | solution.py:60
  18.1 8.6 %collective-permute-start.1 = (bf16[128,1536]{1,0:T(8,128)(2,1)}, bf16[128,1536]{1,0:T(8,128)(2,1)S(1)}, u32[]{:S(2)}, u32[]{:S(2)}) collective-permute-start(bf16[128,1536]{1,0:T(8,128)(2,1)} %param.9), channel_id=1, source_target_pairs={{0,7},{1,0},{2,1},{3,2},{4,3},{5,4},{6,5},{7,6},{8,15},{9,8},{10,9... | collective-permute-start | bytes 1179656 | tf_op jit(solution)/shard_map/ppermute | solution.py:23
  26.7 0.7 copy-start.8
  27.5 320.7 %all-gather.33.cloned.1.call-start = ((), (), s32[]{:S(2)}) async-start(), calls=%async_computation.6 | async-start | bytes 6684672 | tf_op jit(solution)/shard_map/all_gather | solution.py:98
  28.1 373.4 %all-gather.35.cloned.1.call-start = ((), (), s32[]{:S(2)}) async-start(), calls=%async_computation.7 | async-start | bytes 6684672 | tf_op jit(solution)/shard_map/all_gather | solution.py:100
  28.1 8.7 %collective-permute-start.4 = (bf16[128,1536]{1,0:T(8,128)(2,1)}, bf16[128,1536]{1,0:T(8,128)(2,1)S(1)}, u32[]{:S(2)}, u32[]{:S(2)}) collective-permute-start(bf16[128,1536]{1,0:T(8,128)(2,1)} %param.11), channel_id=1, source_target_pairs={{0,1},{1,2},{2,3},{3,4},{4,5},{5,6},{6,7},{7,0},{8,9},{9,10},{10,1... | collective-permute-start | bytes 1179656 | tf_op jit(solution)/shard_map/ppermute | solution.py:23
  36.8 0.7 copy-start.7
  37.6 448.9 %all-gather.29.cloned.1.call-start = ((), (), s32[]{:S(2)}) async-start(), calls=%async_computation.4 | async-start | bytes 6684672 | tf_op jit(solution)/shard_map/all_gather | solution.py:97
  42.4 104.8 %all-to-all-start = ((bf16[16,128,1536]{2,1,0:T(8,128)(2,1)}), bf16[16,128,1536]{2,1,0:T(8,128)(2,1)}, u32[]{:S(2)}, u32[]{:S(2)}) async-start(bf16[16,128,1536]{2,1,0:T(8,128)(2,1)} %concatenate.21), calls=%async_computation | async-start | bytes 12582912 | tf_op jit(solution)/shard_map/all_to_all | solution.py:14
  49.5 479.0 %all-gather.31.cloned.1.call-start = ((), (), s32[]{:S(2)}) async-start(), calls=%async_computation.5 | async-start | bytes 6684672 | tf_op jit(solution)/shard_map/all_gather | solution.py:99
  49.6 8.4 %collective-permute-start.2 = (bf16[128,1536]{1,0:T(8,128)(2,1)S(1)}, bf16[128,1536]{1,0:T(8,128)(2,1)S(1)}, u32[]{:S(2)}, u32[]{:S(2)}) collective-permute-start(bf16[128,1536]{1,0:T(8,128)(2,1)S(1)} %copy-done.5), channel_id=1, source_target_pairs={{0,1},{1,2},{2,3},{3,4},{4,5},{5,6},{6,7},{7,0},{8,9},{9,10},{10,1... | collective-permute-start | bytes 1179656 | tf_op jit(solution)/shard_map/ppermute | solution.py:23
  58.0 0.7 copy-start.9
  330.4 263.4 %collective-permute-start.3 = (f32[12,128]{1,0:T(8,128)S(1)}, f32[12,128]{1,0:T(8,128)S(1)}, u32[]{:S(2)}, u32[]{:S(2)}) collective-permute-start(f32[12,128]{1,0:T(8,128)S(1)} %log_add_fusion), channel_id=1, source_target_pairs={{0,1},{1,2},{2,3},{3,4},{4,5},{5,6},{6,7},{7,0},{8,9},{9,10},{10,1... | collective-permute-start | bytes 18440 | tf_op jit(solution)/shard_map/ppermute | solution.py:23
  346.5 269.0 %collective-permute-start.5 = (f32[12,128]{1,0:T(8,128)S(1)}, f32[12,128]{1,0:T(8,128)S(1)}, u32[]{:S(2)}, u32[]{:S(2)}) collective-permute-start(f32[12,128]{1,0:T(8,128)S(1)} %bitcast.139), channel_id=1, source_target_pairs={{0,1},{1,2},{2,3},{3,4},{4,5},{5,6},{6,7},{7,0},{8,9},{9,10},{10,1... | collective-permute-start | bytes 18440 | tf_op jit(solution)/shard_map/ppermute | solution.py:23
  674.7 12.6 %copy-start.1 = (f32[1000,12]{0,1:T(8,128)S(1)}, f32[1000,12]{0,1:T(8,128)}, u32[]{:S(2)}) copy-start(f32[1000,12]{0,1:T(8,128)} %param.15) | copy-start | bytes 144004
Sparse Core Ops, SparseCore 0:
  17.4 121.3 all-gather.22
  141.0 70.5 all-gather.24
  214.3 60.8 all-gather.26
  277.1 60.8 all-gather.32
  340.6 60.8 all-gather.34
  403.4 61.4 all-gather.28
  467.6 60.8 all-gather.30
